TPU v7x, 768 devices: a whole 4x8x12 slice. The times are simulated.
768 devices in a mesh: segment: 2 (over core), lon: 48 (over y_hi, z), lat: 8 (over y_lo, x).
Axes of the slice: x: 4, y: 8 (y_hi: 4, y_lo: 2; y = y_hi * 2 + y_lo), z: 12, core: 2. Of those that a mesh axis runs over, the one named last changes fastest.
Arguments:
- dec_cot: bfloat16 [2, 768, 192, 128], P('segment', 'lon', 'lat'), may hold values from -6 to 6
- saved_conv: bfloat16 [2, 4, 768, 192, 256], P('segment', None, 'lon', 'lat'), may hold values from -6 to 6
- dec_weight: bfloat16 [256, 128], replicated, may hold values from -0.5 to 0.5
- w_in: bfloat16 [4, 256, 512], replicated, may hold values from -0.375 to 0.375
- w_out: bfloat16 [4, 512, 256], replicated, may hold values from -0.25 to 0.25
- conv_taps: float32 [4, 5, 256], replicated, may hold values from -3 to 3
- dilation: int32 [4], replicated, may hold values from 1 to 48, as said below
Outputs:
- in_adjoint: bfloat16 [2, 768, 192, 256], P('segment', 'lon', 'lat')
Inputs may be any that keep to these rules, and one draw needn't show every extreme that they name: Every layer's dilation lies in 1 to 48; at least one layer has exactly 48.
All inputs are finite; a program needn't handle non-finite values.
Results may differ from a plain program's by a relative error of at most 0.013.
Values may be sent and summed in bfloat16 or wider, within the bound.
A program may use at most 32 MiB of HBM per device.

v0:
```python
import jax
import jax.numpy as jnp
from jax import lax
from jax.sharding import PartitionSpec as P


def with_halo(cells, sides, width):
    for axis, dim in sides:
        count = lax.axis_size(axis)
        ends = count - 1
        head = lax.slice_in_dim(cells, 0, width, axis=dim)
        tail = lax.slice_in_dim(cells, cells.shape[dim] - width, cells.shape[dim], axis=dim)
        cells = jnp.concatenate(
            [
                lax.ppermute(tail, axis, [(i, (i + 1) % count) for i in range(ends)]),
                cells,
                lax.ppermute(head, axis, [((i + 1) % count, i) for i in range(ends)]),
            ],
            axis=dim,
        )
    return cells


def from_behind(value, axis, steps):
    count = lax.axis_size(axis)
    pairs = [(source, (source + steps) % count) for source in range(count)]
    return lax.ppermute(value, axis, pairs)


def partner(block, axis, stride):
    count = lax.axis_size(axis)
    route = []
    for low in range(count):
        high = low | 1 << stride
        if high != low and high < count:
            route += [(low, high), (high, low)]
    return lax.ppermute(block, axis, route)


def gelu_slope(hidden):
    normal_cdf = 0.5 * (1.0 + jax.scipy.special.erf(hidden * 0.7071067811865476))
    density = jnp.exp(-0.5 * hidden * hidden) * 0.3989422804014327
    return normal_cdf + hidden * density


def tap_adjoint(conv_grad, taps_now, offset):
    lon_cells, lat_rows, chans = conv_grad.shape
    lat_padded = with_halo(conv_grad, (("lat", 1),), 1)
    meridional = taps_now[3] * lat_padded[:, 2:] + taps_now[4] * lat_padded[:, :-2]
    centre = taps_now[1] * conv_grad
    rim_width = 3 * lon_cells
    pieces = []
    for distance in (3, 2, 1, 0, -1, -2, -3):
        if distance == 0:
            pieces.append(conv_grad)
        else:
            pieces.append(from_behind(conv_grad, "lon", distance))
    padded = jnp.concatenate(pieces, axis=0)
    ahead_cells = lax.dynamic_slice_in_dim(padded, rim_width + offset, lon_cells, 0)
    behind = lax.dynamic_slice_in_dim(padded, rim_width - offset, lon_cells, 0)
    zonal_sum = taps_now[0] * ahead_cells + taps_now[2] * behind
    zonal_sum = lax.optimization_barrier(zonal_sum.astype(jnp.bfloat16)).astype(jnp.float32)
    return zonal_sum + centre + meridional


def per_device(dec_cot, saved_conv, dec_weight, w_in, w_out, conv_taps, dilation):
    lon_cells = saved_conv.shape[2]
    lat_rows = saved_conv.shape[3]
    chans = saved_conv.shape[4]
    layer_count = w_in.shape[0]
    own_cot = dec_cot[0].reshape(-1, dec_cot.shape[3])
    projected = jnp.einsum(
        "nv,cv->nc", own_cot, dec_weight, preferred_element_type=jnp.float32
    ).astype(jnp.bfloat16)
    handed = partner(projected, "segment", 0)
    gradient = lax.optimization_barrier(handed).astype(jnp.float32)
    for layer_index in reversed(range(layer_count)):
        conv_out = saved_conv[0, layer_index].reshape(-1, chans)
        hidden = jnp.dot(conv_out, w_in[layer_index], preferred_element_type=jnp.float32)
        cot_low = gradient.astype(jnp.bfloat16)
        act_grad = jnp.einsum(
            "nc,hc->nh", cot_low, w_out[layer_index], preferred_element_type=jnp.float32
        )
        pre_grad = (act_grad * gelu_slope(hidden)).astype(jnp.bfloat16)
        conv_grad = jnp.einsum(
            "nh,ch->nc", pre_grad, w_in[layer_index], preferred_element_type=jnp.float32
        ).astype(jnp.bfloat16)
        tapped = tap_adjoint(
            conv_grad.reshape(lon_cells, lat_rows, chans),
            conv_taps[layer_index],
            dilation[layer_index],
        )
        gradient = gradient + tapped.reshape(-1, chans)
    return gradient.reshape(1, lon_cells, lat_rows, chans).astype(jnp.bfloat16)


def solution(mesh):
    in_specs = (
        P("segment", "lon", "lat", None),
        P("segment", None, "lon", "lat", None),
        P(),
        P(),
        P(),
        P(),
        P(),
    )
    out_specs = P("segment", "lon", "lat", None)
    return jax.shard_map(
        per_device, mesh=mesh, in_specs=in_specs, out_specs=out_specs, check_vma=False
    )
```

profile of v0, /device:TPU:80, one launch (start us, length us, event | category | flops | bytes accessed | tf_op | source)
XLA Modules:
  0.0 227.0 jit_solution(781902601807787486)
XLA Ops:
  22.6 9.1 %collective-permute-start.1 = (bf16[16,24,256]{2,1,0:T(8,128)(2,1)S(1)}, bf16[16,24,256]{2,1,0:T(8,128)(2,1)S(1)}, u32[]{:S(2)}, u32[]{:S(2)}) collective-permute-start(bf16[16,24,256]{2,1,0:T(8,128)(2,1)S(1)} %bitcast.126), channel_id=1, source_target_pairs={{0,24},{8,32},{16,40},{24,48},{32,56},{40,64},{48,72},{56,80},{64,... | collective-permute-start | bytes 589832 | tf_op jit(solution)/shard_map/ppermute | solution.py:27
  31.7 6.1 %collective-permute-start.2 = (bf16[16,24,256]{2,1,0:T(8,128)(2,1)S(1)}, bf16[16,24,256]{2,1,0:T(8,128)(2,1)S(1)}, u32[]{:S(2)}, u32[]{:S(2)}) collective-permute-start(bf16[16,24,256]{2,1,0:T(8,128)(2,1)S(1)} %bitcast.127), channel_id=1, source_target_pairs={{0,16},{8,24},{16,32},{24,40},{32,48},{40,56},{48,64},{56,72},{64,... | collective-permute-start | bytes 589832 | tf_op jit(solution)/shard_map/ppermute | solution.py:27
  37.8 4.0 %collective-permute-start.3 = (bf16[16,24,256]{2,1,0:T(8,128)(2,1)S(1)}, bf16[16,24,256]{2,1,0:T(8,128)(2,1)S(1)}, u32[]{:S(2)}, u32[]{:S(2)}) collective-permute-start(bf16[16,24,256]{2,1,0:T(8,128)(2,1)S(1)} %bitcast.128), channel_id=1, source_target_pairs={{0,8},{8,16},{16,24},{24,32},{32,40},{40,48},{48,56},{56,64},{64,7... | collective-permute-start | bytes 589832 | tf_op jit(solution)/shard_map/ppermute | solution.py:27
  43.7 4.0 %collective-permute-start.5 = (bf16[16,24,256]{2,1,0:T(8,128)(2,1)S(1)}, bf16[16,24,256]{2,1,0:T(8,128)(2,1)S(1)}, u32[]{:S(2)}, u32[]{:S(2)}) collective-permute-start(bf16[16,24,256]{2,1,0:T(8,128)(2,1)S(1)} %bitcast.130), channel_id=1, source_target_pairs={{0,368},{8,376},{16,0},{24,8},{32,16},{40,24},{48,32},{56,40},{64,... | collective-permute-start | bytes 589832 | tf_op jit(solution)/shard_map/ppermute | solution.py:27
  47.7 8.8 %collective-permute-done.1 = bf16[16,24,256]{2,1,0:T(8,128)(2,1)S(1)} collective-permute-done((bf16[16,24,256]{2,1,0:T(8,128)(2,1)S(1)}, bf16[16,24,256]{2,1,0:T(8,128)(2,1)S(1)}, u32[]{:S(2)}, u32[]{:S(2)}) %collective-permute-start.1) | collective-permute-done | bytes 196640 | tf_op jit(solution)/shard_map/ppermute | solution.py:27
  62.7 4.5 %collective-permute-start.8 = (bf16[16,1,256]{2,1,0:T(2,128)(2,1)S(1)}, bf16[16,1,256]{2,1,0:T(2,128)(2,1)S(1)}, u32[]{:S(2)}, u32[]{:S(2)}) collective-permute-start(bf16[16,1,256]{2,1,0:T(2,128)(2,1)S(1)} %get-tuple-element.16), channel_id=1, source_target_pairs={{0,1},{1,2},{2,3},{3,4},{4,5},{5,6},{6,7},{8,9},{9,10},{10,11},{11... | collective-permute-start | bytes 24584 | tf_op jit(solution)/shard_map/ppermute | solution.py:15
  67.4 7.7 %collective-permute-done.6 = bf16[16,24,256]{2,1,0:T(8,128)(2,1)S(1)} collective-permute-done((bf16[16,24,256]{2,1,0:T(8,128)(2,1)S(1)}, bf16[16,24,256]{2,1,0:T(8,128)(2,1)S(1)}, u32[]{:S(2)}, u32[]{:S(2)}) %collective-permute-start.6) | collective-permute-done | bytes 196640 | tf_op jit(solution)/shard_map/ppermute | solution.py:27
  88.8 6.6 %collective-permute-start.13 = (bf16[16,24,256]{2,1,0:T(8,128)(2,1)S(1)}, bf16[16,24,256]{2,1,0:T(8,128)(2,1)S(1)}, u32[]{:S(2)}, u32[]{:S(2)}) collective-permute-start(bf16[16,24,256]{2,1,0:T(8,128)(2,1)S(1)} %bitcast.121), channel_id=1, source_target_pairs={{0,368},{8,376},{16,0},{24,8},{32,16},{40,24},{48,32},{56,40},{64,... | collective-permute-start | bytes 589832 | tf_op jit(solution)/shard_map/ppermute | solution.py:27
  98.1 6.3 %collective-permute-start.14 = (bf16[16,24,256]{2,1,0:T(8,128)(2,1)S(1)}, bf16[16,24,256]{2,1,0:T(8,128)(2,1)S(1)}, u32[]{:S(2)}, u32[]{:S(2)}) collective-permute-start(bf16[16,24,256]{2,1,0:T(8,128)(2,1)S(1)} %bitcast.123), channel_id=1, source_target_pairs={{0,360},{8,368},{16,376},{24,0},{32,8},{40,16},{48,24},{56,32},{64... | collective-permute-start | bytes 589832 | tf_op jit(solution)/shard_map/ppermute | solution.py:27
  109.2 4.5 %collective-permute-start.16 = (bf16[16,1,256]{2,1,0:T(2,128)(2,1)S(1)}, bf16[16,1,256]{2,1,0:T(2,128)(2,1)S(1)}, u32[]{:S(2)}, u32[]{:S(2)}) collective-permute-start(bf16[16,1,256]{2,1,0:T(2,128)(2,1)S(1)} %get-tuple-element.14), channel_id=1, source_target_pairs={{0,1},{1,2},{2,3},{3,4},{4,5},{5,6},{6,7},{8,9},{9,10},{10,11},{11... | collective-permute-start | bytes 24584 | tf_op jit(solution)/shard_map/ppermute | solution.py:15
  113.8 5.7 %collective-permute-done.13 = bf16[16,24,256]{2,1,0:T(8,128)(2,1)S(1)} collective-permute-done((bf16[16,24,256]{2,1,0:T(8,128)(2,1)S(1)}, bf16[16,24,256]{2,1,0:T(8,128)(2,1)S(1)}, u32[]{:S(2)}, u32[]{:S(2)}) %collective-permute-start.13) | collective-permute-done | bytes 196640 | tf_op jit(solution)/shard_map/ppermute | solution.py:27
  119.6 7.3 %collective-permute-done.14 = bf16[16,24,256]{2,1,0:T(8,128)(2,1)S(1)} collective-permute-done((bf16[16,24,256]{2,1,0:T(8,128)(2,1)S(1)}, bf16[16,24,256]{2,1,0:T(8,128)(2,1)S(1)}, u32[]{:S(2)}, u32[]{:S(2)}) %collective-permute-start.14) | collective-permute-done | bytes 196640 | tf_op jit(solution)/shard_map/ppermute | solution.py:27
  132.6 6.2 %collective-permute-start.18 = (bf16[16,24,256]{2,1,0:T(8,128)(2,1)S(1)}, bf16[16,24,256]{2,1,0:T(8,128)(2,1)S(1)}, u32[]{:S(2)}, u32[]{:S(2)}) collective-permute-start(bf16[16,24,256]{2,1,0:T(8,128)(2,1)S(1)} %bitcast.136), channel_id=1, source_target_pairs={{0,16},{8,24},{16,32},{24,40},{32,48},{40,56},{48,64},{56,72},{64,... | collective-permute-start | bytes 589832 | tf_op jit(solution)/shard_map/ppermute | solution.py:27
  144.6 6.3 %collective-permute-start.21 = (bf16[16,24,256]{2,1,0:T(8,128)(2,1)S(1)}, bf16[16,24,256]{2,1,0:T(8,128)(2,1)S(1)}, u32[]{:S(2)}, u32[]{:S(2)}) collective-permute-start(bf16[16,24,256]{2,1,0:T(8,128)(2,1)S(1)} %bitcast.139), channel_id=1, source_target_pairs={{0,368},{8,376},{16,0},{24,8},{32,16},{40,24},{48,32},{56,40},{64,... | collective-permute-start | bytes 589832 | tf_op jit(solution)/shard_map/ppermute | solution.py:27
  151.0 4.3 %collective-permute-start.22 = (bf16[16,24,256]{2,1,0:T(8,128)(2,1)S(1)}, bf16[16,24,256]{2,1,0:T(8,128)(2,1)S(1)}, u32[]{:S(2)}, u32[]{:S(2)}) collective-permute-start(bf16[16,24,256]{2,1,0:T(8,128)(2,1)S(1)} %bitcast.141), channel_id=1, source_target_pairs={{0,360},{8,368},{16,376},{24,0},{32,8},{40,16},{48,24},{56,32},{64... | collective-permute-start | bytes 589832 | tf_op jit(solution)/shard_map/ppermute | solution.py:27
  160.5 4.5 %collective-permute-start.24 = (bf16[16,1,256]{2,1,0:T(2,128)(2,1)S(1)}, bf16[16,1,256]{2,1,0:T(2,128)(2,1)S(1)}, u32[]{:S(2)}, u32[]{:S(2)}) collective-permute-start(bf16[16,1,256]{2,1,0:T(2,128)(2,1)S(1)} %get-tuple-element.12), channel_id=1, source_target_pairs={{0,1},{1,2},{2,3},{3,4},{4,5},{5,6},{6,7},{8,9},{9,10},{10,11},{11... | collective-permute-start | bytes 24584 | tf_op jit(solution)/shard_map/ppermute | solution.py:15
  167.8 3.9 %collective-permute-done.22 = bf16[16,24,256]{2,1,0:T(8,128)(2,1)S(1)} collective-permute-done((bf16[16,24,256]{2,1,0:T(8,128)(2,1)S(1)}, bf16[16,24,256]{2,1,0:T(8,128)(2,1)S(1)}, u32[]{:S(2)}, u32[]{:S(2)}) %collective-permute-start.22) | collective-permute-done | bytes 196640 | tf_op jit(solution)/shard_map/ppermute | solution.py:27
  173.6 4.9 %collective-permute-start.25 = (bf16[16,24,256]{2,1,0:T(8,128)(2,1)S(1)}, bf16[16,24,256]{2,1,0:T(8,128)(2,1)S(1)}, u32[]{:S(2)}, u32[]{:S(2)}) collective-permute-start(bf16[16,24,256]{2,1,0:T(8,128)(2,1)S(1)} %bitcast.108), channel_id=1, source_target_pairs={{0,24},{8,32},{16,40},{24,48},{32,56},{40,64},{48,72},{56,80},{64,... | collective-permute-start | bytes 589832 | tf_op jit(solution)/shard_map/ppermute | solution.py:27
  178.5 7.4 %collective-permute-start.26 = (bf16[16,24,256]{2,1,0:T(8,128)(2,1)S(1)}, bf16[16,24,256]{2,1,0:T(8,128)(2,1)S(1)}, u32[]{:S(2)}, u32[]{:S(2)}) collective-permute-start(bf16[16,24,256]{2,1,0:T(8,128)(2,1)S(1)} %bitcast.109), channel_id=1, source_target_pairs={{0,16},{8,24},{16,32},{24,40},{32,48},{40,56},{48,64},{56,72},{64,... | collective-permute-start | bytes 589832 | tf_op jit(solution)/shard_map/ppermute | solution.py:27
  187.8 3.9 %collective-permute-start.28 = (bf16[16,24,256]{2,1,0:T(8,128)(2,1)S(1)}, bf16[16,24,256]{2,1,0:T(8,128)(2,1)S(1)}, u32[]{:S(2)}, u32[]{:S(2)}) collective-permute-start(bf16[16,24,256]{2,1,0:T(8,128)(2,1)S(1)} %bitcast.111), channel_id=1, source_target_pairs={{0,376},{8,0},{16,8},{24,16},{32,24},{40,32},{48,40},{56,48},{64,5... | collective-permute-start | bytes 589832 | tf_op jit(solution)/shard_map/ppermute | solution.py:27
  194.5 4.3 %collective-permute-start.30 = (bf16[16,24,256]{2,1,0:T(8,128)(2,1)S(1)}, bf16[16,24,256]{2,1,0:T(8,128)(2,1)S(1)}, u32[]{:S(2)}, u32[]{:S(2)}) collective-permute-start(bf16[16,24,256]{2,1,0:T(8,128)(2,1)S(1)} %bitcast.114), channel_id=1, source_target_pairs={{0,360},{8,368},{16,376},{24,0},{32,8},{40,16},{48,24},{56,32},{64... | collective-permute-start | bytes 589832 | tf_op jit(solution)/shard_map/ppermute | solution.py:27
  198.8 4.4 %collective-permute-done.26 = bf16[16,24,256]{2,1,0:T(8,128)(2,1)S(1)} collective-permute-done((bf16[16,24,256]{2,1,0:T(8,128)(2,1)S(1)}, bf16[16,24,256]{2,1,0:T(8,128)(2,1)S(1)}, u32[]{:S(2)}, u32[]{:S(2)}) %collective-permute-start.26) | collective-permute-done | bytes 196640 | tf_op jit(solution)/shard_map/ppermute | solution.py:27
  204.5 6.4 %collective-permute-start.32 = (bf16[16,1,256]{2,1,0:T(2,128)(2,1)S(1)}, bf16[16,1,256]{2,1,0:T(2,128)(2,1)S(1)}, u32[]{:S(2)}, u32[]{:S(2)}) collective-permute-start(bf16[16,1,256]{2,1,0:T(2,128)(2,1)S(1)} %get-tuple-element.10), channel_id=1, source_target_pairs={{0,1},{1,2},{2,3},{3,4},{4,5},{5,6},{6,7},{8,9},{9,10},{10,11},{11... | collective-permute-start | bytes 24584 | tf_op jit(solution)/shard_map/ppermute | solution.py:15
  214.8 11.1 %collective-permute-done.30 = bf16[16,24,256]{2,1,0:T(8,128)(2,1)S(1)} collective-permute-done((bf16[16,24,256]{2,1,0:T(8,128)(2,1)S(1)}, bf16[16,24,256]{2,1,0:T(8,128)(2,1)S(1)}, u32[]{:S(2)}, u32[]{:S(2)}) %collective-permute-start.30) | collective-permute-done | bytes 196640 | tf_op jit(solution)/shard_map/ppermute | solution.py:27
  (121 shorter events, 73.8 us)
Async XLA Ops:
  22.6 33.9 %collective-permute-start.1 = (bf16[16,24,256]{2,1,0:T(8,128)(2,1)S(1)}, bf16[16,24,256]{2,1,0:T(8,128)(2,1)S(1)}, u32[]{:S(2)}, u32[]{:S(2)}) collective-permute-start(bf16[16,24,256]{2,1,0:T(8,128)(2,1)S(1)} %bitcast.126), channel_id=1, source_target_pairs={{0,24},{8,32},{16,40},{24,48},{32,56},{40,64},{48,72},{56,80},{64,... | collective-permute-start | bytes 589832 | tf_op jit(solution)/shard_map/ppermute | solution.py:27
  31.7 29.7 %collective-permute-start.2 = (bf16[16,24,256]{2,1,0:T(8,128)(2,1)S(1)}, bf16[16,24,256]{2,1,0:T(8,128)(2,1)S(1)}, u32[]{:S(2)}, u32[]{:S(2)}) collective-permute-start(bf16[16,24,256]{2,1,0:T(8,128)(2,1)S(1)} %bitcast.127), channel_id=1, source_target_pairs={{0,16},{8,24},{16,32},{24,40},{32,48},{40,56},{48,64},{56,72},{64,... | collective-permute-start | bytes 589832 | tf_op jit(solution)/shard_map/ppermute | solution.py:27
  37.8 25.0 %collective-permute-start.3 = (bf16[16,24,256]{2,1,0:T(8,128)(2,1)S(1)}, bf16[16,24,256]{2,1,0:T(8,128)(2,1)S(1)}, u32[]{:S(2)}, u32[]{:S(2)}) collective-permute-start(bf16[16,24,256]{2,1,0:T(8,128)(2,1)S(1)} %bitcast.128), channel_id=1, source_target_pairs={{0,8},{8,16},{16,24},{24,32},{32,40},{40,48},{48,56},{56,64},{64,7... | collective-permute-start | bytes 589832 | tf_op jit(solution)/shard_map/ppermute | solution.py:27
  41.8 25.6 %collective-permute-start.4 = (bf16[16,24,256]{2,1,0:T(8,128)(2,1)S(1)}, bf16[16,24,256]{2,1,0:T(8,128)(2,1)S(1)}, u32[]{:S(2)}, u32[]{:S(2)}) collective-permute-start(bf16[16,24,256]{2,1,0:T(8,128)(2,1)S(1)} %bitcast.129), channel_id=1, source_target_pairs={{0,376},{8,0},{16,8},{24,16},{32,24},{40,32},{48,40},{56,48},{64,5... | collective-permute-start | bytes 589832 | tf_op jit(solution)/shard_map/ppermute | solution.py:27
  43.7 23.7 %collective-permute-start.5 = (bf16[16,24,256]{2,1,0:T(8,128)(2,1)S(1)}, bf16[16,24,256]{2,1,0:T(8,128)(2,1)S(1)}, u32[]{:S(2)}, u32[]{:S(2)}) collective-permute-start(bf16[16,24,256]{2,1,0:T(8,128)(2,1)S(1)} %bitcast.130), channel_id=1, source_target_pairs={{0,368},{8,376},{16,0},{24,8},{32,16},{40,24},{48,32},{56,40},{64,... | collective-permute-start | bytes 589832 | tf_op jit(solution)/shard_map/ppermute | solution.py:27
  77.8 20.3 %collective-permute-start.9 = (bf16[16,24,256]{2,1,0:T(8,128)(2,1)S(1)}, bf16[16,24,256]{2,1,0:T(8,128)(2,1)S(1)}, u32[]{:S(2)}, u32[]{:S(2)}) collective-permute-start(bf16[16,24,256]{2,1,0:T(8,128)(2,1)S(1)} %bitcast.117), channel_id=1, source_target_pairs={{0,24},{8,32},{16,40},{24,48},{32,56},{40,64},{48,72},{56,80},{64,... | collective-permute-start | bytes 589832 | tf_op jit(solution)/shard_map/ppermute | solution.py:27
  79.7 28.1 %collective-permute-start.10 = (bf16[16,24,256]{2,1,0:T(8,128)(2,1)S(1)}, bf16[16,24,256]{2,1,0:T(8,128)(2,1)S(1)}, u32[]{:S(2)}, u32[]{:S(2)}) collective-permute-start(bf16[16,24,256]{2,1,0:T(8,128)(2,1)S(1)} %bitcast.118), channel_id=1, source_target_pairs={{0,16},{8,24},{16,32},{24,40},{32,48},{40,56},{48,64},{56,72},{64,... | collective-permute-start | bytes 589832 | tf_op jit(solution)/shard_map/ppermute | solution.py:27
  82.5 26.7 %collective-permute-start.11 = (bf16[16,24,256]{2,1,0:T(8,128)(2,1)S(1)}, bf16[16,24,256]{2,1,0:T(8,128)(2,1)S(1)}, u32[]{:S(2)}, u32[]{:S(2)}) collective-permute-start(bf16[16,24,256]{2,1,0:T(8,128)(2,1)S(1)} %bitcast.119), channel_id=1, source_target_pairs={{0,8},{8,16},{16,24},{24,32},{32,40},{40,48},{48,56},{56,64},{64,7... | collective-permute-start | bytes 589832 | tf_op jit(solution)/shard_map/ppermute | solution.py:27
  85.4 28.4 %collective-permute-start.12 = (bf16[16,24,256]{2,1,0:T(8,128)(2,1)S(1)}, bf16[16,24,256]{2,1,0:T(8,128)(2,1)S(1)}, u32[]{:S(2)}, u32[]{:S(2)}) collective-permute-start(bf16[16,24,256]{2,1,0:T(8,128)(2,1)S(1)} %bitcast.120), channel_id=1, source_target_pairs={{0,376},{8,0},{16,8},{24,16},{32,24},{40,32},{48,40},{56,48},{64,5... | collective-permute-start | bytes 589832 | tf_op jit(solution)/shard_map/ppermute | solution.py:27
  88.8 30.8 %collective-permute-start.13 = (bf16[16,24,256]{2,1,0:T(8,128)(2,1)S(1)}, bf16[16,24,256]{2,1,0:T(8,128)(2,1)S(1)}, u32[]{:S(2)}, u32[]{:S(2)}) collective-permute-start(bf16[16,24,256]{2,1,0:T(8,128)(2,1)S(1)} %bitcast.121), channel_id=1, source_target_pairs={{0,368},{8,376},{16,0},{24,8},{32,16},{40,24},{48,32},{56,40},{64,... | collective-permute-start | bytes 589832 | tf_op jit(solution)/shard_map/ppermute | solution.py:27
  98.1 28.7 %collective-permute-start.14 = (bf16[16,24,256]{2,1,0:T(8,128)(2,1)S(1)}, bf16[16,24,256]{2,1,0:T(8,128)(2,1)S(1)}, u32[]{:S(2)}, u32[]{:S(2)}) collective-permute-start(bf16[16,24,256]{2,1,0:T(8,128)(2,1)S(1)} %bitcast.123), channel_id=1, source_target_pairs={{0,360},{8,368},{16,376},{24,0},{32,8},{40,16},{48,24},{56,32},{64... | collective-permute-start | bytes 589832 | tf_op jit(solution)/shard_map/ppermute | solution.py:27
  129.1 21.9 %collective-permute-start.17 = (bf16[16,24,256]{2,1,0:T(8,128)(2,1)S(1)}, bf16[16,24,256]{2,1,0:T(8,128)(2,1)S(1)}, u32[]{:S(2)}, u32[]{:S(2)}) collective-permute-start(bf16[16,24,256]{2,1,0:T(8,128)(2,1)S(1)} %bitcast.135), channel_id=1, source_target_pairs={{0,24},{8,32},{16,40},{24,48},{32,56},{40,64},{48,72},{56,80},{64,... | collective-permute-start | bytes 589832 | tf_op jit(solution)/shard_map/ppermute | solution.py:27
  132.6 26.6 %collective-permute-start.18 = (bf16[16,24,256]{2,1,0:T(8,128)(2,1)S(1)}, bf16[16,24,256]{2,1,0:T(8,128)(2,1)S(1)}, u32[]{:S(2)}, u32[]{:S(2)}) collective-permute-start(bf16[16,24,256]{2,1,0:T(8,128)(2,1)S(1)} %bitcast.136), channel_id=1, source_target_pairs={{0,16},{8,24},{16,32},{24,40},{32,48},{40,56},{48,64},{56,72},{64,... | collective-permute-start | bytes 589832 | tf_op jit(solution)/shard_map/ppermute | solution.py:27
  138.7 21.7 %collective-permute-start.19 = (bf16[16,24,256]{2,1,0:T(8,128)(2,1)S(1)}, bf16[16,24,256]{2,1,0:T(8,128)(2,1)S(1)}, u32[]{:S(2)}, u32[]{:S(2)}) collective-permute-start(bf16[16,24,256]{2,1,0:T(8,128)(2,1)S(1)} %bitcast.137), channel_id=1, source_target_pairs={{0,8},{8,16},{16,24},{24,32},{32,40},{40,48},{48,56},{56,64},{64,7... | collective-permute-start | bytes 589832 | tf_op jit(solution)/shard_map/ppermute | solution.py:27
  140.9 24.1 %collective-permute-start.20 = (bf16[16,24,256]{2,1,0:T(8,128)(2,1)S(1)}, bf16[16,24,256]{2,1,0:T(8,128)(2,1)S(1)}, u32[]{:S(2)}, u32[]{:S(2)}) collective-permute-start(bf16[16,24,256]{2,1,0:T(8,128)(2,1)S(1)} %bitcast.138), channel_id=1, source_target_pairs={{0,376},{8,0},{16,8},{24,16},{32,24},{40,32},{48,40},{56,48},{64,5... | collective-permute-start | bytes 589832 | tf_op jit(solution)/shard_map/ppermute | solution.py:27
  144.6 23.2 %collective-permute-start.21 = (bf16[16,24,256]{2,1,0:T(8,128)(2,1)S(1)}, bf16[16,24,256]{2,1,0:T(8,128)(2,1)S(1)}, u32[]{:S(2)}, u32[]{:S(2)}) collective-permute-start(bf16[16,24,256]{2,1,0:T(8,128)(2,1)S(1)} %bitcast.139), channel_id=1, source_target_pairs={{0,368},{8,376},{16,0},{24,8},{32,16},{40,24},{48,32},{56,40},{64,... | collective-permute-start | bytes 589832 | tf_op jit(solution)/shard_map/ppermute | solution.py:27
  151.0 20.8 %collective-permute-start.22 = (bf16[16,24,256]{2,1,0:T(8,128)(2,1)S(1)}, bf16[16,24,256]{2,1,0:T(8,128)(2,1)S(1)}, u32[]{:S(2)}, u32[]{:S(2)}) collective-permute-start(bf16[16,24,256]{2,1,0:T(8,128)(2,1)S(1)} %bitcast.141), channel_id=1, source_target_pairs={{0,360},{8,368},{16,376},{24,0},{32,8},{40,16},{48,24},{56,32},{64... | collective-permute-start | bytes 589832 | tf_op jit(solution)/shard_map/ppermute | solution.py:27
  173.6 20.9 %collective-permute-start.25 = (bf16[16,24,256]{2,1,0:T(8,128)(2,1)S(1)}, bf16[16,24,256]{2,1,0:T(8,128)(2,1)S(1)}, u32[]{:S(2)}, u32[]{:S(2)}) collective-permute-start(bf16[16,24,256]{2,1,0:T(8,128)(2,1)S(1)} %bitcast.108), channel_id=1, source_target_pairs={{0,24},{8,32},{16,40},{24,48},{32,56},{40,64},{48,72},{56,80},{64,... | collective-permute-start | bytes 589832 | tf_op jit(solution)/shard_map/ppermute | solution.py:27
  178.5 24.7 %collective-permute-start.26 = (bf16[16,24,256]{2,1,0:T(8,128)(2,1)S(1)}, bf16[16,24,256]{2,1,0:T(8,128)(2,1)S(1)}, u32[]{:S(2)}, u32[]{:S(2)}) collective-permute-start(bf16[16,24,256]{2,1,0:T(8,128)(2,1)S(1)} %bitcast.109), channel_id=1, source_target_pairs={{0,16},{8,24},{16,32},{24,40},{32,48},{40,56},{48,64},{56,72},{64,... | collective-permute-start | bytes 589832 | tf_op jit(solution)/shard_map/ppermute | solution.py:27
  187.8 23.1 %collective-permute-start.28 = (bf16[16,24,256]{2,1,0:T(8,128)(2,1)S(1)}, bf16[16,24,256]{2,1,0:T(8,128)(2,1)S(1)}, u32[]{:S(2)}, u32[]{:S(2)}) collective-permute-start(bf16[16,24,256]{2,1,0:T(8,128)(2,1)S(1)} %bitcast.111), channel_id=1, source_target_pairs={{0,376},{8,0},{16,8},{24,16},{32,24},{40,32},{48,40},{56,48},{64,5... | collective-permute-start | bytes 589832 | tf_op jit(solution)/shard_map/ppermute | solution.py:27
  191.8 23.0 %collective-permute-start.29 = (bf16[16,24,256]{2,1,0:T(8,128)(2,1)S(1)}, bf16[16,24,256]{2,1,0:T(8,128)(2,1)S(1)}, u32[]{:S(2)}, u32[]{:S(2)}) collective-permute-start(bf16[16,24,256]{2,1,0:T(8,128)(2,1)S(1)} %bitcast.112), channel_id=1, source_target_pairs={{0,368},{8,376},{16,0},{24,8},{32,16},{40,24},{48,32},{56,40},{64,... | collective-permute-start | bytes 589832 | tf_op jit(solution)/shard_map/ppermute | solution.py:27
  194.5 31.4 %collective-permute-start.30 = (bf16[16,24,256]{2,1,0:T(8,128)(2,1)S(1)}, bf16[16,24,256]{2,1,0:T(8,128)(2,1)S(1)}, u32[]{:S(2)}, u32[]{:S(2)}) collective-permute-start(bf16[16,24,256]{2,1,0:T(8,128)(2,1)S(1)} %bitcast.114), channel_id=1, source_target_pairs={{0,360},{8,368},{16,376},{24,0},{32,8},{40,16},{48,24},{56,32},{64... | collective-permute-start | bytes 589832 | tf_op jit(solution)/shard_map/ppermute | solution.py:27
  203.2 22.9 %collective-permute-start.31 = (bf16[16,1,256]{2,1,0:T(2,128)(2,1)S(1)}, bf16[16,1,256]{2,1,0:T(2,128)(2,1)S(1)}, u32[]{:S(2)}, u32[]{:S(2)}) collective-permute-start(bf16[16,1,256]{2,1,0:T(2,128)(2,1)S(1)} %get-tuple-element.9), channel_id=1, source_target_pairs={{1,0},{2,1},{3,2},{4,3},{5,4},{6,5},{7,6},{9,8},{10,9},{11,10},{12... | collective-permute-start | bytes 24584 | tf_op jit(solution)/shard_map/ppermute | solution.py:17
  204.5 21.5 %collective-permute-start.32 = (bf16[16,1,256]{2,1,0:T(2,128)(2,1)S(1)}, bf16[16,1,256]{2,1,0:T(2,128)(2,1)S(1)}, u32[]{:S(2)}, u32[]{:S(2)}) collective-permute-start(bf16[16,1,256]{2,1,0:T(2,128)(2,1)S(1)} %get-tuple-element.10), channel_id=1, source_target_pairs={{0,1},{1,2},{2,3},{3,4},{4,5},{5,6},{6,7},{8,9},{9,10},{10,11},{11... | collective-permute-start | bytes 24584 | tf_op jit(solution)/shard_map/ppermute | solution.py:15
  (20 other events, 339.6 us)
where the time goes:
time: 228 us; the launch traced here: 227 us
  starting transfers between devices  130 us (57%)
  waiting for transfers between devices  67 us (29%)
  between operations  11 us (5%)
  matrix products  10.5 us (5%)
  local copies, waits for them, and re-layouts  5.39 us (2%)
  other arithmetic  2.72 us (1%)
    ppermute x24, starting transfers between devices, from_behind(): return lax.ppermute(value, axis, pairs)  103 us
    ppermute x24, waiting for transfers between devices, from_behind(): return lax.ppermute(value, axis, pairs)  66.9 us
    ppermute x4, starting transfers between devices, with_halo(): lax.ppermute(tail, axis, [(i, (i + 1) % count) for i in range(ends)])  20 us
    dot_general x4, matrix products, per_device(): jnp.einsum('nh,ch->nc', pre_grad, w_in[layer_index], preferred_element_ty...  6.62 us
    ppermute x4, starting transfers between devices, with_halo(): lax.ppermute(head, axis, [((i + 1) % count, i) for i in range(ends)])  5.12 us
  transfers between devices with their start and end apart: 33, of which 13 were waited for; matrix products, arithmetic and copies ran while one was open for 3% of the time, Pallas kernels for 0%

commit v1 on v0

v1 whole, which is shorter than its diff:
```python
import functools

import jax
import jax.numpy as jnp
from jax import lax
from jax.experimental import pallas as pl
from jax.experimental.pallas import tpu as pltpu
from jax.sharding import PartitionSpec as P

MESH = pl.DeviceIdType.MESH
ROWS = 8
PIECES = 2


def gelu_slope(hidden):
    normal_cdf = 0.5 * (1.0 + lax.erf(hidden * 0.7071067811865476))
    density = jnp.exp(-0.5 * hidden * hidden) * 0.3989422804014327
    return normal_cdf + hidden * density


def against(left, right):
    return lax.dot_general(
        left, right, (((1,), (1,)), ((), ())), preferred_element_type=jnp.float32
    )


def hop_cells(reach, cells):
    counts = []
    while reach > 0:
        counts.append(min(reach, cells))
        reach -= cells
    return counts


def kernel(
    dims,
    reaches,
    dilation_ref,
    dec_cot_ref,
    saved_ref,
    dec_weight_ref,
    w_in_ref,
    w_out_ref,
    taps_ref,
    out_ref,
    *scratch,
):
    layers, cells, lats, chans, hidden_units, lon_count, lat_count = dims
    chunks = lats // ROWS
    zonal = [scratch[l * chunks : (l + 1) * chunks] for l in range(layers)]
    (
        ahead_halo,
        behind_halo,
        dec_here,
        dec_weight,
        saved,
        w_in,
        w_out,
        slope,
        grad,
        load_sem,
        dec_sem,
        hop_send,
        hop_recv,
        lat_send,
        lat_recv,
    ) = scratch[layers * chunks :]

    seg = lax.axis_index("segment")
    lon = lax.axis_index("lon")
    lat = lax.axis_index("lat")
    east = lax.rem(lon + 1, lon_count)
    west = lax.rem(lon + lon_count - 1, lon_count)
    north = lax.rem(lat + 1, lat_count)
    south = lax.rem(lat + lat_count - 1, lat_count)

    barrier = pltpu.get_barrier_semaphore()
    for peer in (
        {"segment": 1 - seg},
        {"lon": east},
        {"lon": west},
        {"lat": north},
        {"lat": south},
    ):
        pl.semaphore_signal(barrier, inc=1, device_id=peer, device_id_type=MESH)

    loads = {}

    def load(name, src, dst):
        loads[name] = pltpu.make_async_copy(src, dst, load_sem.at[len(loads)])
        loads[name].start()

    for l in reversed(range(layers)):
        load(("saved", l), saved_ref.at[l], saved.at[l])
        load(("w_in", l), w_in_ref.at[l], w_in.at[l])
        if l == layers - 1:
            load("dec_weight", dec_weight_ref, dec_weight)
        load(("w_out", l), w_out_ref.at[l], w_out.at[l])

    def slope_piece(l, piece):
        if piece == 0:
            loads["saved", l].wait()
            loads["w_in", l].wait()
        span = cells // PIECES
        rows = span * lats
        hidden = jnp.dot(
            saved[l, pl.ds(piece * rows, rows), :],
            w_in[l],
            preferred_element_type=jnp.float32,
        )
        slope[l, pl.ds(piece * span, span)] = gelu_slope(hidden).reshape(
            span, lats, hidden_units
        )

    pl.semaphore_wait(barrier, 5)
    dec_copy = pltpu.make_async_remote_copy(
        src_ref=dec_cot_ref,
        dst_ref=dec_here,
        send_sem=dec_sem.at[0],
        recv_sem=dec_sem.at[1],
        device_id={"segment": 1 - seg},
        device_id_type=MESH,
    )
    dec_copy.start()
    for piece in range(PIECES):
        slope_piece(layers - 1, piece)
    loads["dec_weight"].wait()
    dec_copy.wait()
    handed = against(dec_here[...], dec_weight[...]).astype(jnp.bfloat16)
    grad[...] = handed.astype(jnp.float32).reshape(cells, lats, chans)

    hop_copies = {}

    def start_hop(l, c, hop):
        counts = hop_cells(reaches[l], cells)
        if hop >= len(counts):
            return
        count, reach, buf = counts[hop], reaches[l], zonal[l][c]
        hops = len(counts)
        slot = (l * chunks + c) * 6 + hop * 2
        own = reach + hop * cells
        to_west = pltpu.make_async_remote_copy(
            src_ref=buf.at[pl.ds(own, count)],
            dst_ref=buf.at[pl.ds(own + cells, count)],
            send_sem=hop_send.at[slot],
            recv_sem=hop_recv.at[slot],
            device_id={"lon": west},
            device_id_type=MESH,
        )
        own = reach - hop * cells + cells - count
        to_east = pltpu.make_async_remote_copy(
            src_ref=buf.at[pl.ds(own, count)],
            dst_ref=buf.at[pl.ds(own - cells, count)],
            send_sem=hop_send.at[slot + 1],
            recv_sem=hop_recv.at[slot + 1],
            device_id={"lon": east},
            device_id_type=MESH,
        )
        to_west.start()
        to_east.start()
        hop_copies[l, c, hop] = (to_west, to_east)

    def arrive(l, c, hop):
        for copy in hop_copies.get((l, c, hop), ()):
            copy.wait_recv()

    lat_copies = {}

    def start_lat(l, c):
        own = zonal[l][c].at[pl.ds(reaches[l], cells)]
        for which, chunk, peer, halo in (
            (0, 0, south, ahead_halo),
            (1, chunks - 1, north, behind_halo),
        ):
            if c == chunk:
                copy = pltpu.make_async_remote_copy(
                    src_ref=own,
                    dst_ref=halo.at[l],
                    send_sem=lat_send.at[2 * l + which],
                    recv_sem=lat_recv.at[2 * l + which],
                    device_id={"lat": peer},
                    device_id_type=MESH,
                )
                copy.start()
                lat_copies[l, which] = copy

    def conv_grad(l, c):
        if c == 0:
            loads["w_out", l].wait()
        rows = pl.ds(c * ROWS, ROWS)
        low = grad[:, rows, :].reshape(cells * ROWS, chans).astype(jnp.bfloat16)
        act = against(low, w_out[l])
        steep = slope[l, :, rows, :].reshape(cells * ROWS, hidden_units)
        pre = (act * steep).astype(jnp.bfloat16)
        result = against(pre, w_in[l]).reshape(cells, ROWS, chans)
        zonal[l][c][pl.ds(reaches[l], cells)] = result.astype(jnp.bfloat16)
        start_hop(l, c, 0)
        start_lat(l, c)

    def field(l, c):
        return zonal[l][c][pl.ds(reaches[l], cells)].astype(jnp.float32)

    def tapped(l, c):
        taps = [taps_ref[t, l, :].reshape(1, 1, chans) for t in range(5)]
        offset = dilation_ref[l]
        reach = reaches[l]
        place = lax.broadcasted_iota(jnp.int32, (cells, ROWS, chans), 1)
        here = field(l, c)
        if c + 1 < chunks:
            after = field(l, c + 1)
        else:
            after = ahead_halo[l].astype(jnp.float32)
            after = jnp.where(lat == lat_count - 1, jnp.zeros_like(after), after)
        if c > 0:
            before = field(l, c - 1)
        else:
            before = behind_halo[l].astype(jnp.float32)
            before = jnp.where(lat == 0, jnp.zeros_like(before), before)
        next_row = pltpu.roll(jnp.where(place == 0, after, here), ROWS - 1, 1)
        last_row = pltpu.roll(jnp.where(place == ROWS - 1, before, here), 1, 1)
        window = zonal[l][c]
        ahead = window[pl.ds(reach + offset, cells)].astype(jnp.float32)
        behind = window[pl.ds(reach - offset, cells)].astype(jnp.float32)
        both = (taps[0] * ahead + taps[2] * behind).astype(jnp.bfloat16)
        return (
            both.astype(jnp.float32)
            + taps[1] * here
            + (taps[3] * next_row + taps[4] * last_row)
        )

    for c in range(chunks):
        conv_grad(layers - 1, c)

    for l in reversed(range(layers)):
        hops = len(hop_cells(reaches[l], cells))
        for c in range(chunks):
            arrive(l, c, 0)
            start_hop(l, c, 1)
            if l > 0 and c < PIECES:
                slope_piece(l - 1, c)
        for hop in range(1, hops - 1):
            for c in range(chunks):
                arrive(l, c, hop)
                start_hop(l, c, hop + 1)
        for which in (1, 0):
            lat_copies[l, which].wait_recv()
        for c in range(chunks):
            if hops > 1:
                arrive(l, c, hops - 1)
            rows = pl.ds(c * ROWS, ROWS)
            total = grad[:, rows, :] + tapped(l, c)
            if l > 0:
                grad[:, rows, :] = total
                conv_grad(l - 1, c)
            else:
                out_ref[:, rows, :] = total.astype(jnp.bfloat16)

    for copies in hop_copies.values():
        for copy in copies:
            copy.wait_send()
    for copy in lat_copies.values():
        copy.wait_send()


def whole_block(dims, reaches, *operands):
    layers, cells, lats, chans, hidden_units, _, _ = dims
    chunks = lats // ROWS
    dec_rows, values = operands[1].shape
    bf16, f32 = jnp.bfloat16, jnp.float32
    anywhere = pl.BlockSpec(memory_space=pl.ANY)
    return pl.pallas_call(
        functools.partial(kernel, dims, reaches),
        out_shape=jax.ShapeDtypeStruct((cells, lats, chans), bf16),
        in_specs=[
            pl.BlockSpec(memory_space=pltpu.SMEM),
            anywhere,
            anywhere,
            anywhere,
            anywhere,
            anywhere,
            pl.BlockSpec(memory_space=pltpu.VMEM),
        ],
        out_specs=pl.BlockSpec(memory_space=pltpu.VMEM),
        scratch_shapes=[
            pltpu.VMEM((cells + 2 * reaches[l], ROWS, chans), bf16)
            for l in range(layers)
            for c in range(chunks)
        ]
        + [
            pltpu.VMEM((layers, cells, ROWS, chans), bf16),
            pltpu.VMEM((layers, cells, ROWS, chans), bf16),
            pltpu.VMEM((dec_rows, values), bf16),
            pltpu.VMEM((chans, values), bf16),
            pltpu.VMEM((layers, cells * lats, chans), bf16),
            pltpu.VMEM((layers, chans, hidden_units), bf16),
            pltpu.VMEM((layers, hidden_units, chans), bf16),
            pltpu.VMEM((layers, cells, lats, hidden_units), f32),
            pltpu.VMEM((cells, lats, chans), f32),
            pltpu.SemaphoreType.DMA((3 * layers + 1,)),
            pltpu.SemaphoreType.DMA((2,)),
            pltpu.SemaphoreType.DMA((6 * layers * chunks,)),
            pltpu.SemaphoreType.DMA((6 * layers * chunks,)),
            pltpu.SemaphoreType.DMA((2 * layers,)),
            pltpu.SemaphoreType.DMA((2 * layers,)),
        ],
        compiler_params=pltpu.CompilerParams(
            collective_id=0, has_side_effects=True, vmem_limit_bytes=60 << 20
        ),
    )(*operands)


def solution(mesh):
    lon_count, lat_count = mesh.shape["lon"], mesh.shape["lat"]

    def per_device(dec_cot, saved_conv, dec_weight, w_in, w_out, conv_taps, dilation):
        _, layers, cells, lats, chans = saved_conv.shape
        hidden_units = w_in.shape[2]
        dims = (layers, cells, lats, chans, hidden_units, lon_count, lat_count)
        reaches = (3 * cells,) * layers
        out = whole_block(
            dims,
            reaches,
            dilation,
            dec_cot[0].reshape(cells * lats, -1),
            saved_conv[0].reshape(layers, cells * lats, chans),
            dec_weight,
            w_in,
            w_out,
            conv_taps.transpose(1, 0, 2),
        )
        return out[None]

    in_specs = (
        P("segment", "lon", "lat", None),
        P("segment", None, "lon", "lat", None),
        P(),
        P(),
        P(),
        P(),
        P(),
    )
    out_specs = P("segment", "lon", "lat", None)
    return jax.shard_map(
        per_device, mesh=mesh, in_specs=in_specs, out_specs=out_specs, check_vma=False
    )
```

time: 228 us -> 171 us (0.75)
  the two profiles are of different devices: /device:TPU:80 before, /device:TPU:62 now
where the time goes in v1:
time: 171 us; the launch traced here: 170 us
  Pallas kernels  169 us (99%)
    pallas_call x1, Pallas kernels, whole_block(): pl.pallas_call(functools.partial(kernel, dims, reaches), out_shape=jax.Sh...  169 us

profile of v1, /device:TPU:62, one launch (start us, length us, event | category | flops | bytes accessed | tf_op | source)
XLA Modules:
  0.0 170.5 jit_solution(1313005430470967715)
XLA Ops:
  0.0 168.9 %shard_map.73 = bf16[16,24,256]{2,1,0:T(8,128)(2,1)} custom-call(s32[4]{0:T(128)} %dilation_ref.1, bf16[384,128]{1,0:T(8,128)(2,1)} %bitcast.6, bf16[4,384,256]{2,1,0:T(8,128)(2,1)} %bitcast.4, bf16[256,128]{1,0:T(8,128)(2,1)} %dec_weight_ref.1, bf16[4,256,512]{2,1,0:T(8,128)(2,1)} %w_in_ref.1, bf16[4,512,256]{2,1,0:T(8,128)(2,1)} %w_out_ref.1, ...), custom_call_target="tpu_custom_call" | custom-call | tf_op jit(solution)/shard_map/pallas_call | solution.py:271
  168.9 1.6 copy.9

commit v2 on v1

--- a/solution.py
+++ b/solution.py
@@ -9,6 +9,8 @@
 
 MESH = pl.DeviceIdType.MESH
 ROWS = 8
+RING = 12
+LAG = 2
 PIECES = 2
 
 
@@ -49,8 +51,8 @@
     chunks = lats // ROWS
     zonal = [scratch[l * chunks : (l + 1) * chunks] for l in range(layers)]
     (
-        ahead_halo,
-        behind_halo,
+        edge,
+        halo,
         dec_here,
         dec_weight,
         saved,
@@ -62,6 +64,7 @@
         dec_sem,
         hop_send,
         hop_recv,
+        via_send,
         lat_send,
         lat_recv,
     ) = scratch[layers * chunks :]
@@ -74,6 +77,15 @@
     north = lax.rem(lat + 1, lat_count)
     south = lax.rem(lat + lat_count - 1, lat_count)
 
+    def along(steps):
+        return lax.rem(lon + lon_count + steps, lon_count)
+
+    place_in_row = lax.rem(lon, RING)
+    turns = lat // (lat_count // 2)
+    turns_east = turns * (place_in_row // (RING - 1))
+    turns_west = turns * ((RING - 1 - place_in_row) // (RING - 1))
+    next_row, last_row = along(RING), along(-RING)
+
     barrier = pltpu.get_barrier_semaphore()
     for peer in (
         {"segment": 1 - seg},
@@ -81,6 +93,10 @@
         {"lon": west},
         {"lat": north},
         {"lat": south},
+        {"lon": next_row},
+        {"lon": last_row},
+        {"lon": along(RING - 1)},
+        {"lon": along(1 - RING)},
     ):
         pl.semaphore_signal(barrier, inc=1, device_id=peer, device_id_type=MESH)
 
@@ -112,7 +128,7 @@
             span, lats, hidden_units
         )
 
-    pl.semaphore_wait(barrier, 5)
+    pl.semaphore_wait(barrier, 9)
     dec_copy = pltpu.make_async_remote_copy(
         src_ref=dec_cot_ref,
         dst_ref=dec_here,
@@ -129,53 +145,78 @@
     handed = against(dec_here[...], dec_weight[...]).astype(jnp.bfloat16)
     grad[...] = handed.astype(jnp.float32).reshape(cells, lats, chans)
 
-    hop_copies = {}
-
-    def start_hop(l, c, hop):
-        counts = hop_cells(reaches[l], cells)
-        if hop >= len(counts):
-            return
-        count, reach, buf = counts[hop], reaches[l], zonal[l][c]
-        hops = len(counts)
-        slot = (l * chunks + c) * 6 + hop * 2
-        own = reach + hop * cells
-        to_west = pltpu.make_async_remote_copy(
+    order = [c for c in range(chunks) if 0 < c < chunks - 1] + [chunks - 1, 0]
+    sent = []
+    quick = place_in_row // (RING // 2)
+    sides = (quick, 1 - quick)
+
+    def hop_count(l):
+        return len(hop_cells(reaches[l], cells))
+
+    def slot_of(l, c, hop):
+        return (l * chunks + c) * 3 + hop
+
+    def either(choice, one, other):
+        return other + choice * (one - other)
+
+    def hop_copy(l, c, hop, side, turn):
+        count, buf = hop_cells(reaches[l], cells)[hop], zonal[l][c]
+        slot = slot_of(l, c, hop)
+        own = reaches[l] + either(side, cells - count - hop * cells, hop * cells)
+        landing = own + either(side, -cells, cells)
+        via = cells + 2 * reaches[l] + hop * cells
+        straight, round_corner = either(side, east, west), either(side, next_row, last_row)
+        return pltpu.make_async_remote_copy(
             src_ref=buf.at[pl.ds(own, count)],
-            dst_ref=buf.at[pl.ds(own + cells, count)],
-            send_sem=hop_send.at[slot],
-            recv_sem=hop_recv.at[slot],
-            device_id={"lon": west},
+            dst_ref=buf.at[pl.ds(either(turn, via, landing), count)],
+            send_sem=hop_send.at[2 * slot + side],
+            recv_sem=hop_recv.at[
+                either(turn, 6 * layers * chunks + slot, 2 * slot + side)
+            ],
+            device_id={"lon": either(turn, round_corner, straight)},
             device_id_type=MESH,
         )
-        own = reach - hop * cells + cells - count
-        to_east = pltpu.make_async_remote_copy(
-            src_ref=buf.at[pl.ds(own, count)],
-            dst_ref=buf.at[pl.ds(own - cells, count)],
-            send_sem=hop_send.at[slot + 1],
-            recv_sem=hop_recv.at[slot + 1],
-            device_id={"lon": east},
+
+    def turned_copy(l, c, hop):
+        count, buf = hop_cells(reaches[l], cells)[hop], zonal[l][c]
+        slot = slot_of(l, c, hop)
+        via = cells + 2 * reaches[l] + hop * cells
+        landing = reaches[l] + either(turns_east, -count - hop * cells, (hop + 1) * cells)
+        return pltpu.make_async_remote_copy(
+            src_ref=buf.at[pl.ds(via, count)],
+            dst_ref=buf.at[pl.ds(landing, count)],
+            send_sem=via_send.at[slot],
+            recv_sem=hop_recv.at[2 * slot + turns_east],
+            device_id={"lon": along(either(turns_east, 1 - RING, RING - 1))},
             device_id_type=MESH,
         )
-        to_west.start()
-        to_east.start()
-        hop_copies[l, c, hop] = (to_west, to_east)
-
-    def arrive(l, c, hop):
-        for copy in hop_copies.get((l, c, hop), ()):
-            copy.wait_recv()
+
+    def start_hop(l, c, hop, side):
+        copy = hop_copy(l, c, hop, side, either(side, turns_east, turns_west))
+        copy.start()
+        sent.append(copy)
+
+    def arrive(l, c, hop, side):
+        hop_copy(l, c, hop, side, 0).wait_recv()
+
+    def turn_on(l, c, hop):
+        @pl.when(turns_east + turns_west == 1)
+        def _():
+            hop_copy(l, c, hop, turns_east, 1).wait_recv()
+            turned_copy(l, c, hop).start()
 
     lat_copies = {}
 
-    def start_lat(l, c):
-        own = zonal[l][c].at[pl.ds(reaches[l], cells)]
-        for which, chunk, peer, halo in (
-            (0, 0, south, ahead_halo),
-            (1, chunks - 1, north, behind_halo),
+    def start_lat(l, c, result):
+        for which, chunk, row, peer in (
+            (0, 0, 0, south),
+            (1, chunks - 1, ROWS - 1, north),
         ):
             if c == chunk:
+                edge[l, which] = result[:, row, :].astype(jnp.bfloat16)
                 copy = pltpu.make_async_remote_copy(
-                    src_ref=own,
-                    dst_ref=halo.at[l],
+                    src_ref=edge.at[l, which],
+                    dst_ref=halo.at[l, which],
                     send_sem=lat_send.at[2 * l + which],
                     recv_sem=lat_recv.at[2 * l + which],
                     device_id={"lat": peer},
@@ -184,8 +225,14 @@
                 copy.start()
                 lat_copies[l, which] = copy
 
+    def halo_row(l, which, outside):
+        lat_copies[l, which].wait_recv()
+        row = halo[l, which].astype(jnp.float32)
+        row = jnp.where(outside, jnp.zeros_like(row), row)
+        return row.reshape(cells, 1, chans)
+
     def conv_grad(l, c):
-        if c == 0:
+        if c == order[0]:
             loads["w_out", l].wait()
         rows = pl.ds(c * ROWS, ROWS)
         low = grad[:, rows, :].reshape(cells * ROWS, chans).astype(jnp.bfloat16)
@@ -194,8 +241,9 @@
         pre = (act * steep).astype(jnp.bfloat16)
         result = against(pre, w_in[l]).reshape(cells, ROWS, chans)
         zonal[l][c][pl.ds(reaches[l], cells)] = result.astype(jnp.bfloat16)
-        start_hop(l, c, 0)
-        start_lat(l, c)
+        for side in sides:
+            start_hop(l, c, 0, side)
+        start_lat(l, c, result)
 
     def field(l, c):
         return zonal[l][c][pl.ds(reaches[l], cells)].astype(jnp.float32)
@@ -209,15 +257,13 @@
         if c + 1 < chunks:
             after = field(l, c + 1)
         else:
-            after = ahead_halo[l].astype(jnp.float32)
-            after = jnp.where(lat == lat_count - 1, jnp.zeros_like(after), after)
+            after = halo_row(l, 0, lat == lat_count - 1)
         if c > 0:
             before = field(l, c - 1)
         else:
-            before = behind_halo[l].astype(jnp.float32)
-            before = jnp.where(lat == 0, jnp.zeros_like(before), before)
-        next_row = pltpu.roll(jnp.where(place == 0, after, here), ROWS - 1, 1)
-        last_row = pltpu.roll(jnp.where(place == ROWS - 1, before, here), 1, 1)
+            before = halo_row(l, 1, lat == 0)
+        from_north = pltpu.roll(jnp.where(place == 0, after, here), ROWS - 1, 1)
+        from_south = pltpu.roll(jnp.where(place == ROWS - 1, before, here), 1, 1)
         window = zonal[l][c]
         ahead = window[pl.ds(reach + offset, cells)].astype(jnp.float32)
         behind = window[pl.ds(reach - offset, cells)].astype(jnp.float32)
@@ -225,28 +271,35 @@
         return (
             both.astype(jnp.float32)
             + taps[1] * here
-            + (taps[3] * next_row + taps[4] * last_row)
-        )
-
-    for c in range(chunks):
+            + (taps[3] * from_north + taps[4] * from_south)
+        )
+
+    for c in order:
         conv_grad(layers - 1, c)
 
     for l in reversed(range(layers)):
-        hops = len(hop_cells(reaches[l], cells))
-        for c in range(chunks):
-            arrive(l, c, 0)
-            start_hop(l, c, 1)
-            if l > 0 and c < PIECES:
-                slope_piece(l - 1, c)
-        for hop in range(1, hops - 1):
-            for c in range(chunks):
-                arrive(l, c, hop)
-                start_hop(l, c, hop + 1)
-        for which in (1, 0):
-            lat_copies[l, which].wait_recv()
-        for c in range(chunks):
-            if hops > 1:
-                arrive(l, c, hops - 1)
+        last = hop_count(l) - 1
+        pieces = list(range(PIECES)) if l > 0 else []
+        steps = [(hop, c) for hop in range(last) for c in order]
+        ends = [(last, c) for c in order]
+
+        def pass_on(step, side):
+            arrive(l, step[1], step[0], side)
+            start_hop(l, step[1], step[0] + 1, side)
+
+        for i, step in enumerate(steps + ends[:LAG]):
+            if step[0] < last:
+                pass_on(step, sides[0])
+            turn_on(l, step[1], step[0])
+            if 0 <= i - LAG < len(steps):
+                pass_on(steps[i - LAG], sides[1])
+            if pieces and i % 2 == 1:
+                slope_piece(l - 1, pieces.pop(0))
+        for piece in pieces:
+            slope_piece(l - 1, piece)
+        for i, c in enumerate(order):
+            for side in sides:
+                arrive(l, c, last, side)
             rows = pl.ds(c * ROWS, ROWS)
             total = grad[:, rows, :] + tapped(l, c)
             if l > 0:
@@ -254,10 +307,19 @@
                 conv_grad(l - 1, c)
             else:
                 out_ref[:, rows, :] = total.astype(jnp.bfloat16)
-
-    for copies in hop_copies.values():
-        for copy in copies:
-            copy.wait_send()
+            if i + LAG < chunks:
+                turn_on(l, order[i + LAG], last)
+
+    for copy in sent:
+        copy.wait_send()
+
+    @pl.when(turns_east + turns_west == 1)
+    def _():
+        for l in range(layers):
+            for c in range(chunks):
+                for hop in range(hop_count(l)):
+                    turned_copy(l, c, hop).wait_send()
+
     for copy in lat_copies.values():
         copy.wait_send()
 
@@ -282,13 +344,16 @@
         ],
         out_specs=pl.BlockSpec(memory_space=pltpu.VMEM),
         scratch_shapes=[
-            pltpu.VMEM((cells + 2 * reaches[l], ROWS, chans), bf16)
+            pltpu.VMEM(
+                (cells + 2 * reaches[l] + cells * len(hop_cells(reaches[l], cells)), ROWS, chans),
+                bf16,
+            )
             for l in range(layers)
             for c in range(chunks)
         ]
         + [
-            pltpu.VMEM((layers, cells, ROWS, chans), bf16),
-            pltpu.VMEM((layers, cells, ROWS, chans), bf16),
+            pltpu.VMEM((layers, 2, cells, chans), bf16),
+            pltpu.VMEM((layers, 2, cells, chans), bf16),
             pltpu.VMEM((dec_rows, values), bf16),
             pltpu.VMEM((chans, values), bf16),
             pltpu.VMEM((layers, cells * lats, chans), bf16),
@@ -299,7 +364,8 @@
             pltpu.SemaphoreType.DMA((3 * layers + 1,)),
             pltpu.SemaphoreType.DMA((2,)),
             pltpu.SemaphoreType.DMA((6 * layers * chunks,)),
-            pltpu.SemaphoreType.DMA((6 * layers * chunks,)),
+            pltpu.SemaphoreType.DMA((9 * layers * chunks,)),
+            pltpu.SemaphoreType.DMA((3 * layers * chunks,)),
             pltpu.SemaphoreType.DMA((2 * layers,)),
             pltpu.SemaphoreType.DMA((2 * layers,)),
         ],

time: 171 us -> 104 us (0.61)
  the two profiles are of different devices: /device:TPU:62 before, /device:TPU:8 now
where the time goes in v2:
time: 104 us; the launch traced here: 103 us
  Pallas kernels  102 us (98%)
  local copies, waits for them, and re-layouts  1.62 us (2%)
    pallas_call x1, Pallas kernels, whole_block(): pl.pallas_call(functools.partial(kernel, dims, reaches), out_shape=jax.Sh...  102 us

profile of v2, /device:TPU:8, one launch (start us, length us, event | category | flops | bytes accessed | tf_op | source)
XLA Modules:
  0.0 103.3 jit_solution(11598187381767437954)
XLA Ops:
  0.0 101.7 %shard_map.73 = bf16[16,24,256]{2,1,0:T(8,128)(2,1)} custom-call(s32[4]{0:T(128)} %dilation_ref.1, bf16[384,128]{1,0:T(8,128)(2,1)} %bitcast.6, bf16[4,384,256]{2,1,0:T(8,128)(2,1)} %bitcast.4, bf16[256,128]{1,0:T(8,128)(2,1)} %dec_weight_ref.1, bf16[4,256,512]{2,1,0:T(8,128)(2,1)} %w_in_ref.1, bf16[4,512,256]{2,1,0:T(8,128)(2,1)} %w_out_ref.1, ...), custom_call_target="tpu_custom_call" | custom-call | tf_op jit(solution)/shard_map/pallas_call | solution.py:333
  101.7 1.6 %copy.9 = bf16[1,16,24,256]{3,2,1,0:T(8,128)(2,1)} copy(bf16[1,16,24,256]{3,2,1,0:T(8,128)(2,1)} %bitcast.5) | data formatting | bytes 393216

commit v3 on v2

--- a/solution.py
+++ b/solution.py
@@ -10,7 +10,8 @@
 MESH = pl.DeviceIdType.MESH
 ROWS = 8
 RING = 12
-LAG = 2
+LAG = 3
+LEAD = 2
 PIECES = 2
 
 
@@ -84,6 +85,7 @@
     turns = lat // (lat_count // 2)
     turns_east = turns * (place_in_row // (RING - 1))
     turns_west = turns * ((RING - 1 - place_in_row) // (RING - 1))
+    at_end = place_in_row // (RING - 1) + (RING - 1 - place_in_row) // (RING - 1)
     next_row, last_row = along(RING), along(-RING)
 
     barrier = pltpu.get_barrier_semaphore()
@@ -146,7 +148,6 @@
     grad[...] = handed.astype(jnp.float32).reshape(cells, lats, chans)
 
     order = [c for c in range(chunks) if 0 < c < chunks - 1] + [chunks - 1, 0]
-    sent = []
     quick = place_in_row // (RING // 2)
     sides = (quick, 1 - quick)
 
@@ -192,9 +193,7 @@
         )
 
     def start_hop(l, c, hop, side):
-        copy = hop_copy(l, c, hop, side, either(side, turns_east, turns_west))
-        copy.start()
-        sent.append(copy)
+        hop_copy(l, c, hop, side, either(side, turns_east, turns_west)).start()
 
     def arrive(l, c, hop, side):
         hop_copy(l, c, hop, side, 0).wait_recv()
@@ -287,16 +286,21 @@
             arrive(l, step[1], step[0], side)
             start_hop(l, step[1], step[0] + 1, side)
 
-        for i, step in enumerate(steps + ends[:LAG]):
-            if step[0] < last:
-                pass_on(step, sides[0])
-            turn_on(l, step[1], step[0])
-            if 0 <= i - LAG < len(steps):
-                pass_on(steps[i - LAG], sides[1])
-            if pieces and i % 2 == 1:
-                slope_piece(l - 1, pieces.pop(0))
         for piece in pieces:
             slope_piece(l - 1, piece)
+        events = list(enumerate(steps + ends[:LEAD] + [None] * LAG))
+
+        def relay(lag):
+            for i, step in events:
+                if step is not None:
+                    if step[0] < last:
+                        pass_on(step, sides[0])
+                    turn_on(l, step[1], step[0])
+                if 0 <= i - lag < len(steps):
+                    pass_on(steps[i - lag], sides[1])
+
+        pl.when(at_end == 1)(functools.partial(relay, LAG))
+        pl.when(at_end == 0)(functools.partial(relay, 0))
         for i, c in enumerate(order):
             for side in sides:
                 arrive(l, c, last, side)
@@ -307,11 +311,14 @@
                 conv_grad(l - 1, c)
             else:
                 out_ref[:, rows, :] = total.astype(jnp.bfloat16)
-            if i + LAG < chunks:
-                turn_on(l, order[i + LAG], last)
-
-    for copy in sent:
-        copy.wait_send()
+            if i + LEAD < chunks:
+                turn_on(l, order[i + LEAD], last)
+
+    for l in range(layers):
+        for c in range(chunks):
+            for hop in range(hop_count(l)):
+                for side in range(2):
+                    hop_copy(l, c, hop, side, 0).wait_send()
 
     @pl.when(turns_east + turns_west == 1)
     def _():

time: 104 us -> 100 us (0.962)
  Pallas kernels: 102 us -> 98.2 us
    pallas_call x1, Pallas kernels: 102 us -> 98.2 us  [whole_block(): pl.pallas_call(functools.partial(kernel, dims, reaches), out_shape=jax.Sh...]
where the time goes in v3:
time: 100 us; the launch traced here: 99.9 us
  Pallas kernels  98.2 us (98%)
  local copies, waits for them, and re-layouts  1.62 us (2%)
    pallas_call x1, Pallas kernels, whole_block(): pl.pallas_call(functools.partial(kernel, dims, reaches), out_shape=jax.Sh...  98.2 us

profile of v3, /device:TPU:8, one launch (start us, length us, event | category | flops | bytes accessed | tf_op | source)
XLA Modules:
  0.0 99.9 jit_solution(11843881111285469997)
XLA Ops:
  0.0 98.2 %shard_map.73 = bf16[16,24,256]{2,1,0:T(8,128)(2,1)} custom-call(s32[4]{0:T(128)} %dilation_ref.1, bf16[384,128]{1,0:T(8,128)(2,1)} %bitcast.6, bf16[4,384,256]{2,1,0:T(8,128)(2,1)} %bitcast.4, bf16[256,128]{1,0:T(8,128)(2,1)} %dec_weight_ref.1, bf16[4,256,512]{2,1,0:T(8,128)(2,1)} %w_in_ref.1, bf16[4,512,256]{2,1,0:T(8,128)(2,1)} %w_out_ref.1, ...), custom_call_target="tpu_custom_call" | custom-call | tf_op jit(solution)/shard_map/pallas_call | solution.py:340
  98.2 1.6 %copy.9 = bf16[1,16,24,256]{3,2,1,0:T(8,128)(2,1)} copy(bf16[1,16,24,256]{3,2,1,0:T(8,128)(2,1)} %bitcast.5) | data formatting | bytes 393216

commit v4 on v3

--- a/solution.py
+++ b/solution.py
@@ -10,7 +10,7 @@
 MESH = pl.DeviceIdType.MESH
 ROWS = 8
 RING = 12
-LAG = 3
+LAG = 4
 LEAD = 2
 PIECES = 2
 
@@ -82,7 +82,7 @@
         return lax.rem(lon + lon_count + steps, lon_count)
 
     place_in_row = lax.rem(lon, RING)
-    turns = lat // (lat_count // 2)
+    turns = seg
     turns_east = turns * (place_in_row // (RING - 1))
     turns_west = turns * ((RING - 1 - place_in_row) // (RING - 1))
     at_end = place_in_row // (RING - 1) + (RING - 1 - place_in_row) // (RING - 1)

time: 100 us -> 98.2 us (0.982)
  the two profiles are of different devices: /device:TPU:8 before, /device:TPU:1 now
where the time goes in v4:
time: 98.2 us; the launch traced here: 98 us
  Pallas kernels  96.4 us (98%)
  local copies, waits for them, and re-layouts  1.62 us (2%)
    pallas_call x1, Pallas kernels, whole_block(): pl.pallas_call(functools.partial(kernel, dims, reaches), out_shape=jax.Sh...  96.4 us

profile of v4, /device:TPU:1, one launch (start us, length us, event | category | flops | bytes accessed | tf_op | source)
XLA Modules:
  0.0 98.0 jit_solution(9770247237162233174)
XLA Ops:
  0.0 96.4 %shard_map.73 = bf16[16,24,256]{2,1,0:T(8,128)(2,1)} custom-call(s32[4]{0:T(128)} %dilation_ref.1, bf16[384,128]{1,0:T(8,128)(2,1)} %bitcast.6, bf16[4,384,256]{2,1,0:T(8,128)(2,1)} %bitcast.4, bf16[256,128]{1,0:T(8,128)(2,1)} %dec_weight_ref.1, bf16[4,256,512]{2,1,0:T(8,128)(2,1)} %w_in_ref.1, bf16[4,512,256]{2,1,0:T(8,128)(2,1)} %w_out_ref.1, ...), custom_call_target="tpu_custom_call" | custom-call | tf_op jit(solution)/shard_map/pallas_call | solution.py:340
  96.4 1.6 %copy.9 = bf16[1,16,24,256]{3,2,1,0:T(8,128)(2,1)} copy(bf16[1,16,24,256]{3,2,1,0:T(8,128)(2,1)} %bitcast.5) | data formatting | bytes 393216

commit v5 on v4

--- a/solution.py
+++ b/solution.py
@@ -10,7 +10,7 @@
 MESH = pl.DeviceIdType.MESH
 ROWS = 8
 RING = 12
-LAG = 4
+LAG = 5
 LEAD = 2
 PIECES = 2
 

time: 98.2 us -> 99.6 us (1.014)
  Pallas kernels: 96.4 us -> 97.7 us
    pallas_call x1, Pallas kernels: 96.4 us -> 97.7 us  [whole_block(): pl.pallas_call(functools.partial(kernel, dims, reaches), out_shape=jax.Sh...]
where the time goes in v5:
time: 99.6 us; the launch traced here: 99.4 us
  Pallas kernels  97.7 us (98%)
  local copies, waits for them, and re-layouts  1.62 us (2%)
    pallas_call x1, Pallas kernels, whole_block(): pl.pallas_call(functools.partial(kernel, dims, reaches), out_shape=jax.Sh...  97.7 us

profile of v5, /device:TPU:1, one launch (start us, length us, event | category | flops | bytes accessed | tf_op | source)
XLA Modules:
  0.0 99.4 jit_solution(8654468234572732805)
XLA Ops:
  0.0 97.7 %shard_map.73 = bf16[16,24,256]{2,1,0:T(8,128)(2,1)} custom-call(s32[4]{0:T(128)} %dilation_ref.1, bf16[384,128]{1,0:T(8,128)(2,1)} %bitcast.6, bf16[4,384,256]{2,1,0:T(8,128)(2,1)} %bitcast.4, bf16[256,128]{1,0:T(8,128)(2,1)} %dec_weight_ref.1, bf16[4,256,512]{2,1,0:T(8,128)(2,1)} %w_in_ref.1, bf16[4,512,256]{2,1,0:T(8,128)(2,1)} %w_out_ref.1, ...), custom_call_target="tpu_custom_call" | custom-call | tf_op jit(solution)/shard_map/pallas_call | solution.py:340
  97.8 1.6 %copy.9 = bf16[1,16,24,256]{3,2,1,0:T(8,128)(2,1)} copy(bf16[1,16,24,256]{3,2,1,0:T(8,128)(2,1)} %bitcast.5) | data formatting | bytes 393216

commit v6 on v4

--- a/solution.py
+++ b/solution.py
@@ -11,7 +11,7 @@
 ROWS = 8
 RING = 12
 LAG = 4
-LEAD = 2
+LEAD = 3
 PIECES = 2
 
 

time: 98.2 us -> 96.1 us (0.979)
  Pallas kernels: 96.4 us -> 94.5 us
    pallas_call x1, Pallas kernels: 96.4 us -> 94.5 us  [whole_block(): pl.pallas_call(functools.partial(kernel, dims, reaches), out_shape=jax.Sh...]
where the time goes in v6:
time: 96.1 us
  Pallas kernels  94.5 us (98%)
  local copies, waits for them, and re-layouts  1.62 us (2%)
    pallas_call x1, Pallas kernels, whole_block(): pl.pallas_call(functools.partial(kernel, dims, reaches), out_shape=jax.Sh...  94.5 us

profile of v6, /device:TPU:1, one launch (start us, length us, event | category | flops | bytes accessed | tf_op | source)
XLA Modules:
  0.0 96.1 jit_solution(1364366009719478263)
XLA Ops:
  0.0 94.5 %shard_map.73 = bf16[16,24,256]{2,1,0:T(8,128)(2,1)} custom-call(s32[4]{0:T(128)} %dilation_ref.1, bf16[384,128]{1,0:T(8,128)(2,1)} %bitcast.6, bf16[4,384,256]{2,1,0:T(8,128)(2,1)} %bitcast.4, bf16[256,128]{1,0:T(8,128)(2,1)} %dec_weight_ref.1, bf16[4,256,512]{2,1,0:T(8,128)(2,1)} %w_in_ref.1, bf16[4,512,256]{2,1,0:T(8,128)(2,1)} %w_out_ref.1, ...), custom_call_target="tpu_custom_call" | custom-call | tf_op jit(solution)/shard_map/pallas_call | solution.py:340
  94.5 1.6 %copy.9 = bf16[1,16,24,256]{3,2,1,0:T(8,128)(2,1)} copy(bf16[1,16,24,256]{3,2,1,0:T(8,128)(2,1)} %bitcast.5) | data formatting | bytes 393216
